TPU v7x, 128 devices: a whole 4x4x4 slice. The times are simulated.
128 devices in a mesh: band: 32 (over z, x, core), lev: 4 (over y).
Axes of the slice: x: 4, y: 4, z: 4, core: 2. Of those that a mesh axis runs over, the one named last changes fastest.
Arguments:
- air_fourier_coefficients: float32 [4, 16, 1280, 256], P('lev', None, 'band'), may hold values from -6 to 6
- quadrature_factor: float32 [1280], P('band'), may hold values from 0.5 to 1.5
- associated_polynomial_table: bfloat16 [128, 1280, 1280], P('band'), may hold values from -6 to 6
- east_west_harmonic: int32 [128], replicated, may hold values from 0 to 1279, as said below
- boundary_diffusion: float32 [4, 16, 16, 1280], P('lev', None, None, 'band'), may hold values from -0.25 to 0.25
- bulk_transfer_coefficient: float32 [4, 1280], P('lev', 'band'), may hold values from 0.1 to 1
- skin_heat_earlier: float32 [12, 4, 1280, 256], P(None, 'lev', 'band'), may hold values from -6 to 6
- sea_boundary_values: float32 [4, 1024, 1440], P('lev', 'band'), may hold values from -6 to 6
- sea_damping_speed: float32 [4, 1024, 1440], P('lev', 'band'), may hold values from 0.02 to 2
- sea_coupling_matrix: float32 [4, 4], replicated, may hold values from -1.75 to 1.75
- patch_active_entries: int32 [32], P('band'), may hold values from 8 to 32, as said below
- sea_southern_parallel: int32 [1024], P('band'), may hold values from 0 to 1278, as said below
- sea_northern_share: float32 [1024], P('band'), may hold values from 0 to 1
- air_paired_cells: int32 [2, 1280], P(None, 'band'), may hold values from 0 to 1023, as said below
- air_second_share: float32 [1280], P('band'), may hold values from 0 to 1
Outputs:
- air_coefficients_end: float32 [4, 16, 1280, 256], P('lev', None, 'band')
- sea_values_end: float32 [4, 1024, 1440], P('lev', 'band')
- skin_heat_newest: float32 [12, 4, 1280, 256], P(None, 'lev', 'band')
Inputs may be any that keep to these rules, and one draw needn't show every extreme that they name: `east_west_harmonic`: Distinct; positions 2 j and 2 j + 1 hold m and 1279 - m for some m below 640; 0 is among them. `patch_active_entries`: the live slots of a tile come first; the last tile is full. For a slot of tile t, sea_southern_parallel and sea_southern_parallel + 1 lie in t * 40 - 8 to (t + 1) * 40 + 7; they do not decrease along a tile's live slots. `air_paired_cells`: for a latitude of band t both taps are live slots of tiles t - 1, t or t + 1, the first one of tile t, and the two differ.
All inputs are finite; a program needn't handle non-finite values.
Results may differ from a plain program's by a relative error of at most 0.014.
Values may be sent and summed in bfloat16 or wider, within the bound.
No kernel may reach another device: no remote copies, remote signals or barrier semaphores. Data moves between devices by JAX's collectives and lax.ppermute only.
A program may use at most 64 MiB of HBM per device.

v0:
```python
import math
import jax
import jax.numpy as jnp
from jax import lax
from jax.sharding import PartitionSpec as P

PARALLEL_NUMBER = 1280
MARG = 8
degree_damping = 2e-06
ocean_step = 0.5
mixing_diagonal = 0.95
synth_divisor = 4.0


def with_halo(shard, sides, width):
    for axis, dim in sides:
        size, length = (lax.axis_size(axis), shard.shape[dim])
        up = [(i, (i + 1) % size) for i in range(size - 1)]
        down = [(j, i) for i, j in up]
        last = lax.slice_in_dim(shard, length - width, length, axis=dim)
        first = lax.slice_in_dim(shard, 0, width, axis=dim)
        before = lax.ppermute(last, axis, up)
        after = lax.ppermute(first, axis, down)
        shard = jnp.concatenate([before, shard, after], axis=dim)
    return shard


def damping_table(wave_values, degree_count):
    degrees = wave_values[:, None] + jnp.arange(degree_count, dtype=jnp.int32)[None, :]
    degree_float = degrees.astype(jnp.float32)
    factor = 1.0 / (1.0 + degree_damping * degree_float * (degree_float + 1.0))
    return jnp.where(degrees < degree_count, factor, jnp.zeros_like(factor))


def zonal_table(wave_values, lon_count):
    longitude = jnp.arange(lon_count, dtype=jnp.int32)
    phases = wave_values[:, None] * longitude[None, :] % lon_count
    angles = phases.astype(jnp.float32) * (2.0 * math.pi / lon_count)
    stacked = jnp.stack([jnp.cos(angles), -jnp.sin(angles)], axis=1)
    return stacked.reshape(2 * wave_values.shape[0], lon_count).astype(jnp.bfloat16)


def padded_transform(values, tables, damping):
    row_count = values.shape[0]
    lat_count = values.shape[1]
    wave_count = tables.shape[0]
    shaped = values.reshape(row_count, lat_count, wave_count, 2)
    spectral = jnp.einsum("rlmc,mln->rmnc", shaped, tables, preferred_element_type=jnp.float32)
    damped = (spectral * damping[None, :, :, None]).astype(jnp.bfloat16)
    synthesis = jnp.einsum("rmnc,mln->rlmc", damped, tables, preferred_element_type=jnp.float32)
    synthesis = synthesis * (1.0 / (synth_divisor * math.sqrt(tables.shape[2])))
    return synthesis.astype(jnp.bfloat16).reshape(row_count, lat_count, wave_count * 2)


def per_device(
    air_fourier_coefficients,
    quadrature_factor,
    associated_polynomial_table,
    east_west_harmonic,
    boundary_diffusion,
    bulk_transfer_coefficient,
    skin_heat_earlier,
    sea_boundary_values,
    sea_damping_speed,
    sea_coupling_matrix,
    patch_active_entries,
    sea_southern_parallel,
    sea_northern_share,
    air_paired_cells,
    air_second_share,
):
    band_index = lax.axis_index("band")
    lev_index = lax.axis_index("lev")
    field_local = air_fourier_coefficients.shape[0]
    height_pile = air_fourier_coefficients.shape[1]
    lat_local = air_fourier_coefficients.shape[2]
    column_count = air_fourier_coefficients.shape[3]
    row_count = field_local * height_pile
    owned = associated_polynomial_table.shape[0]
    degree_count = associated_polynomial_table.shape[2]
    wave_values = lax.dynamic_slice_in_dim(east_west_harmonic, band_index * owned, owned, 0)
    damping = damping_table(wave_values, degree_count)

    def transform(values):
        return padded_transform(values, associated_polynomial_table, damping)

    identity_block = jnp.eye(height_pile, dtype=jnp.float32)[None, :, :, None]
    mixing = (
        mixing_diagonal * identity_block
        + boundary_diffusion
        - jnp.transpose(boundary_diffusion, (0, 2, 1, 3))
    )
    weight = quadrature_factor * (1.0 / math.sqrt(PARALLEL_NUMBER))

    def march_air_model(air_model_present, skin_heat_present):
        scaled = (air_model_present * weight[None, None, :, None]).astype(jnp.bfloat16)
        scaled = scaled.reshape(row_count, lat_local, column_count)
        by_wave = lax.all_to_all(scaled, "band", split_axis=2, concat_axis=1, tiled=True)
        synthesis = transform(by_wave)
        returned = lax.all_to_all(synthesis, "band", split_axis=1, concat_axis=2, tiled=True)
        synthesis_field = returned.reshape(
            field_local, height_pile, lat_local, column_count
        ).astype(jnp.float32)
        halfway_point = air_model_present - synthesis_field
        bottom_sheet = bulk_transfer_coefficient[:, :, None] * (
            skin_heat_present - halfway_point[:, height_pile - 1]
        )
        mixed_state = jnp.einsum(
            "flpa,fpac->flac", mixing, halfway_point, precision=lax.Precision.HIGHEST
        )
        mixed_state = mixed_state.at[:, height_pile - 1].add(bottom_sheet)
        return (mixed_state, bottom_sheet.astype(jnp.bfloat16))

    air_coefficients_end, forcing_series = lax.scan(
        march_air_model, air_fourier_coefficients, skin_heat_earlier
    )
    slot_rows = sea_boundary_values.shape[1]
    extended = with_halo(forcing_series, (("band", 2),), MARG)
    rim_rows = lat_local + 2 * MARG
    lowest = band_index * lat_local - MARG
    live_slot = jnp.arange(slot_rows, dtype=jnp.int32) < patch_active_entries[0]
    offsets = (sea_southern_parallel - lowest)[:, None]
    rim_index = jnp.arange(rim_rows, dtype=jnp.int32)[None, :]
    low_weight = jnp.where(live_slot, 1.0 - sea_northern_share, jnp.zeros_like(sea_northern_share))[
        :, None
    ]
    high_weight = jnp.where(live_slot, sea_northern_share, jnp.zeros_like(sea_northern_share))[
        :, None
    ]
    flux_taps = jnp.where(rim_index == offsets, low_weight, 0.0) + jnp.where(
        rim_index == offsets + 1, high_weight, 0.0
    )
    flux_taps = flux_taps.astype(jnp.bfloat16)
    ocean_flux = jnp.einsum(
        "sa,kfac->kfsc", flux_taps, extended, preferred_element_type=jnp.float32
    ).astype(jnp.bfloat16)
    lon_count = sea_boundary_values.shape[2]
    zonal_basis = zonal_table(east_west_harmonic, lon_count)
    synth_scale = 1.0 / math.sqrt(zonal_basis.shape[0])
    skew_full = sea_coupling_matrix - sea_coupling_matrix.T
    skew_mine = lax.dynamic_slice_in_dim(skew_full, lev_index * field_local, field_local, 0)

    def ocean_advance(ocean_now, flux_now):
        forcing = (
            jnp.einsum("fsc,cx->fsx", flux_now, zonal_basis, preferred_element_type=jnp.float32)
            * synth_scale
        )
        gathered = lax.all_gather(ocean_now.astype(jnp.bfloat16), "lev", axis=0, tiled=True)
        coupled = jnp.zeros_like(ocean_now)
        for field_index in range(gathered.shape[0]):
            coupled = (
                coupled
                + skew_mine[:, field_index][:, None, None]
                * gathered[field_index].astype(jnp.float32)[None]
            )
        updated = (ocean_now + ocean_step * (coupled - forcing)) / (
            1.0 + ocean_step * sea_damping_speed
        )
        return (updated, updated.astype(jnp.bfloat16))

    sea_values_end, ocean_wave = lax.scan(ocean_advance, sea_boundary_values, ocean_flux)
    ocean_coef = jnp.einsum(
        "kfsx,cx->kfsc", ocean_wave, zonal_basis, preferred_element_type=jnp.float32
    )
    ocean_coef = (ocean_coef * (1.0 / math.sqrt(lon_count))).astype(jnp.bfloat16)
    neighbours = with_halo(ocean_coef, (("band", 2),), slot_rows)
    base_slot = (band_index - 1) * slot_rows
    slot_index = jnp.arange(3 * slot_rows, dtype=jnp.int32)[None, :]
    first_local = (air_paired_cells[0] - base_slot)[:, None]
    second_local = (air_paired_cells[1] - base_slot)[:, None]
    return_taps = jnp.where(
        slot_index == first_local, (1.0 - air_second_share)[:, None], 0.0
    ) + jnp.where(slot_index == second_local, air_second_share[:, None], 0.0)
    return_taps = return_taps.astype(jnp.bfloat16)
    skin_heat_newest = jnp.einsum(
        "ga,kfac->kfgc", return_taps, neighbours, preferred_element_type=jnp.float32
    )
    return (air_coefficients_end, sea_values_end, skin_heat_newest)


def solution(mesh):
    return jax.shard_map(
        per_device,
        mesh=mesh,
        in_specs=(
            P("lev", None, "band", None),
            P("band"),
            P("band", None, None),
            P(),
            P("lev", None, None, "band"),
            P("lev", "band"),
            P(None, "lev", "band", None),
            P("lev", "band", None),
            P("lev", "band", None),
            P(),
            P("band"),
            P("band"),
            P("band"),
            P(None, "band"),
            P("band"),
        ),
        out_specs=(
            P("lev", None, "band", None),
            P("lev", "band", None),
            P(None, "lev", "band", None),
        ),
        check_vma=False,
    )
```

profile of v0, /device:TPU:15, one launch (start us, length us, event | category | flops | bytes accessed | tf_op | source)
XLA Modules:
  0.0 1154.0 jit_solution(6040955849517082085)
XLA Ops:
  4.1 916.9 %while.29 = (s32[]{:T(128)}, f32[1,16,40,256]{3,1,2,0:T(8,128)S(1)}, bf16[12,1,40,256]{3,2,1,0:T(8,128)(2,1)S(1)}, f32[40]{0:T(128)S(1)}, bf16[4,1280,1280]{2,1,...) while((s32[]{:T(128)}, ...), condition=%wide.region_1.2_spmd.clone, body=%wide.region_0.1_spmd.clone.sunk | while | flops 871552000 | bytes 31130164 | solution.py:114
  7.8 8.7 all-to-all-start
  16.6 8.1 all-to-all-done
  28.9 15.2 %fusion.110 = bf16[4,16,2,1280]{3,1,2,0:T(8,128)(2,1)} fusion(bf16[4,1280,1280]{2,1,0:T(8,128)(2,1)} %get-tuple-element.499, bf16[16,1280,4,2]{1,0,3,2:T(8,128)(2,1)S(1)} %reshape.391, f32[4,1280]{1,0:T(4,128)S(1)} %divide_select_fusion.2), kind=kOutput, calls=%fused_computation.17.clone.1 | convolution fusion | flops 839516160 | bytes 13783040 | tf_op jit(solution)/shard_map/while/body/eval_jaxpr/rmnc,mln->rlmc/dot_general | solution.py:50
  58.0 6.2 all-to-all-done.1
  92.6 8.1 all-to-all-done
  105.0 15.2 %fusion.110 = bf16[4,16,2,1280]{3,1,2,0:T(8,128)(2,1)} fusion(bf16[4,1280,1280]{2,1,0:T(8,128)(2,1)} %get-tuple-element.499, bf16[16,1280,4,2]{1,0,3,2:T(8,128)(2,1)S(1)} %reshape.391, f32[4,1280]{1,0:T(4,128)S(1)} %divide_select_fusion.2), kind=kOutput, calls=%fused_computation.17.clone.1 | convolution fusion | flops 839516160 | bytes 13783040 | tf_op jit(solution)/shard_map/while/body/eval_jaxpr/rmnc,mln->rlmc/dot_general | solution.py:50
  134.1 6.2 all-to-all-done.1
  168.8 8.1 all-to-all-done
  181.1 15.2 %fusion.110 = bf16[4,16,2,1280]{3,1,2,0:T(8,128)(2,1)} fusion(bf16[4,1280,1280]{2,1,0:T(8,128)(2,1)} %get-tuple-element.499, bf16[16,1280,4,2]{1,0,3,2:T(8,128)(2,1)S(1)} %reshape.391, f32[4,1280]{1,0:T(4,128)S(1)} %divide_select_fusion.2), kind=kOutput, calls=%fused_computation.17.clone.1 | convolution fusion | flops 839516160 | bytes 13783040 | tf_op jit(solution)/shard_map/while/body/eval_jaxpr/rmnc,mln->rlmc/dot_general | solution.py:50
  244.9 8.1 all-to-all-done
  257.2 15.2 %fusion.110 = bf16[4,16,2,1280]{3,1,2,0:T(8,128)(2,1)} fusion(bf16[4,1280,1280]{2,1,0:T(8,128)(2,1)} %get-tuple-element.499, bf16[16,1280,4,2]{1,0,3,2:T(8,128)(2,1)S(1)} %reshape.391, f32[4,1280]{1,0:T(4,128)S(1)} %divide_select_fusion.2), kind=kOutput, calls=%fused_computation.17.clone.1 | convolution fusion | flops 839516160 | bytes 13783040 | tf_op jit(solution)/shard_map/while/body/eval_jaxpr/rmnc,mln->rlmc/dot_general | solution.py:50
  321.0 8.1 all-to-all-done
  333.3 15.2 %fusion.110 = bf16[4,16,2,1280]{3,1,2,0:T(8,128)(2,1)} fusion(bf16[4,1280,1280]{2,1,0:T(8,128)(2,1)} %get-tuple-element.499, bf16[16,1280,4,2]{1,0,3,2:T(8,128)(2,1)S(1)} %reshape.391, f32[4,1280]{1,0:T(4,128)S(1)} %divide_select_fusion.2), kind=kOutput, calls=%fused_computation.17.clone.1 | convolution fusion | flops 839516160 | bytes 13783040 | tf_op jit(solution)/shard_map/while/body/eval_jaxpr/rmnc,mln->rlmc/dot_general | solution.py:50
  362.4 6.2 all-to-all-done.1
  397.1 8.1 all-to-all-done
  409.4 15.2 %fusion.110 = bf16[4,16,2,1280]{3,1,2,0:T(8,128)(2,1)} fusion(bf16[4,1280,1280]{2,1,0:T(8,128)(2,1)} %get-tuple-element.499, bf16[16,1280,4,2]{1,0,3,2:T(8,128)(2,1)S(1)} %reshape.391, f32[4,1280]{1,0:T(4,128)S(1)} %divide_select_fusion.2), kind=kOutput, calls=%fused_computation.17.clone.1 | convolution fusion | flops 839516160 | bytes 13783040 | tf_op jit(solution)/shard_map/while/body/eval_jaxpr/rmnc,mln->rlmc/dot_general | solution.py:50
  438.5 6.2 all-to-all-done.1
  473.2 8.1 all-to-all-done
  485.5 15.2 %fusion.110 = bf16[4,16,2,1280]{3,1,2,0:T(8,128)(2,1)} fusion(bf16[4,1280,1280]{2,1,0:T(8,128)(2,1)} %get-tuple-element.499, bf16[16,1280,4,2]{1,0,3,2:T(8,128)(2,1)S(1)} %reshape.391, f32[4,1280]{1,0:T(4,128)S(1)} %divide_select_fusion.2), kind=kOutput, calls=%fused_computation.17.clone.1 | convolution fusion | flops 839516160 | bytes 13783040 | tf_op jit(solution)/shard_map/while/body/eval_jaxpr/rmnc,mln->rlmc/dot_general | solution.py:50
  514.6 6.2 all-to-all-done.1
  549.3 8.1 all-to-all-done
  561.6 15.2 %fusion.110 = bf16[4,16,2,1280]{3,1,2,0:T(8,128)(2,1)} fusion(bf16[4,1280,1280]{2,1,0:T(8,128)(2,1)} %get-tuple-element.499, bf16[16,1280,4,2]{1,0,3,2:T(8,128)(2,1)S(1)} %reshape.391, f32[4,1280]{1,0:T(4,128)S(1)} %divide_select_fusion.2), kind=kOutput, calls=%fused_computation.17.clone.1 | convolution fusion | flops 839516160 | bytes 13783040 | tf_op jit(solution)/shard_map/while/body/eval_jaxpr/rmnc,mln->rlmc/dot_general | solution.py:50
  590.7 6.2 all-to-all-done.1
  625.4 8.1 all-to-all-done
  637.7 15.2 %fusion.110 = bf16[4,16,2,1280]{3,1,2,0:T(8,128)(2,1)} fusion(bf16[4,1280,1280]{2,1,0:T(8,128)(2,1)} %get-tuple-element.499, bf16[16,1280,4,2]{1,0,3,2:T(8,128)(2,1)S(1)} %reshape.391, f32[4,1280]{1,0:T(4,128)S(1)} %divide_select_fusion.2), kind=kOutput, calls=%fused_computation.17.clone.1 | convolution fusion | flops 839516160 | bytes 13783040 | tf_op jit(solution)/shard_map/while/body/eval_jaxpr/rmnc,mln->rlmc/dot_general | solution.py:50
  701.5 8.1 all-to-all-done
  713.8 15.2 %fusion.110 = bf16[4,16,2,1280]{3,1,2,0:T(8,128)(2,1)} fusion(bf16[4,1280,1280]{2,1,0:T(8,128)(2,1)} %get-tuple-element.499, bf16[16,1280,4,2]{1,0,3,2:T(8,128)(2,1)S(1)} %reshape.391, f32[4,1280]{1,0:T(4,128)S(1)} %divide_select_fusion.2), kind=kOutput, calls=%fused_computation.17.clone.1 | convolution fusion | flops 839516160 | bytes 13783040 | tf_op jit(solution)/shard_map/while/body/eval_jaxpr/rmnc,mln->rlmc/dot_general | solution.py:50
  777.6 8.1 all-to-all-done
  789.9 15.2 %fusion.110 = bf16[4,16,2,1280]{3,1,2,0:T(8,128)(2,1)} fusion(bf16[4,1280,1280]{2,1,0:T(8,128)(2,1)} %get-tuple-element.499, bf16[16,1280,4,2]{1,0,3,2:T(8,128)(2,1)S(1)} %reshape.391, f32[4,1280]{1,0:T(4,128)S(1)} %divide_select_fusion.2), kind=kOutput, calls=%fused_computation.17.clone.1 | convolution fusion | flops 839516160 | bytes 13783040 | tf_op jit(solution)/shard_map/while/body/eval_jaxpr/rmnc,mln->rlmc/dot_general | solution.py:50
  819.0 6.2 all-to-all-done.1
  853.7 8.1 all-to-all-done
  866.0 15.2 %fusion.110 = bf16[4,16,2,1280]{3,1,2,0:T(8,128)(2,1)} fusion(bf16[4,1280,1280]{2,1,0:T(8,128)(2,1)} %get-tuple-element.499, bf16[16,1280,4,2]{1,0,3,2:T(8,128)(2,1)S(1)} %reshape.391, f32[4,1280]{1,0:T(4,128)S(1)} %divide_select_fusion.2), kind=kOutput, calls=%fused_computation.17.clone.1 | convolution fusion | flops 839516160 | bytes 13783040 | tf_op jit(solution)/shard_map/while/body/eval_jaxpr/rmnc,mln->rlmc/dot_general | solution.py:50
  934.2 169.7 %while.28 = (s32[]{:T(128)}, f32[1,32,1440]{2,1,0:T(8,128)S(1)}, bf16[12,1,32,1440]{3,2,1,0:T(8,128)(2,1)S(1)}, f32[1,4]{1,0:T(1,128)S(1)}, bf16[12,1,32,256]{3,...) while((s32[]{:T(128)}, f32[1,32,1440]{2,1,0:T(8,128)S(1)}, ...), condition=%wide.region_3.4_spmd, body=%wide.region_2.3_spmd.sunk | while | flops 24514560 | bytes 2624629 | solution.py:161
  934.9 9.9 all_gather.4
  949.0 10.5 all_gather.4
  963.7 9.3 all_gather.4
  977.3 9.6 all_gather.4
  991.1 9.6 all_gather.4
  1005.0 10.4 all_gather.4
  1019.6 9.6 all_gather.4
  1033.5 10.5 all_gather.4
  1048.2 9.3 all_gather.4
  1061.7 9.7 all_gather.4
  1075.6 9.6 all_gather.4
  1089.5 10.9 all_gather.4
  1104.4 39.4 %collective-permute-start.2 = (bf16[12,1,32,256]{3,2,0,1:T(8,128)(2,1)S(1)}, bf16[12,1,32,256]{3,2,0,1:T(8,128)(2,1)S(1)}, u32[]{:S(2)}, u32[]{:S(2)}) collective-permute-start(bf16[12,1,32,256]{3,2,0,1:T(8,128)(2,1)S(1)} %fusion.46), channel_id=1, source_target_pairs={{0,4},{4,8},{8,12},{12,16},{16,20},{20,24},{24,28},{28,32},{32,36}... | collective-permute-start | bytes 589832 | tf_op jit(solution)/shard_map/ppermute | solution.py:22
  1146.4 6.5 collective-permute-done.3
  (397 shorter events, 653.0 us)
Async XLA Ops:
  0.6 2.4 copy-start.4
  0.6 2.6 copy-start.12
  0.7 2.6 copy-start.8
  3.0 1.1 copy-start.5
  4.1 926.1 %copy-start.6 = (f32[4,4]{1,0:T(4,128)S(1)}, f32[4,4]{1,0:T(4,128)}, u32[]{:S(2)}) copy-start(f32[4,4]{1,0:T(4,128)} %param.30) | copy-start | bytes 196
  4.1 926.2 %copy-start.9 = (s32[32]{0:T(128)S(1)}, s32[32]{0:T(128)}, u32[]{:S(2)}) copy-start(s32[32]{0:T(128)} %param.32) | copy-start | bytes 388
  4.1 926.2 %copy-start.10 = (f32[32]{0:T(128)S(1)}, f32[32]{0:T(128)}, u32[]{:S(2)}) copy-start(f32[32]{0:T(128)} %param.33) | copy-start | bytes 388
  7.8 16.8 %all-to-all-start = ((bf16[32,2,2560]{2,1,0:T(2,128)(2,1)}), bf16[32,2,2560]{2,1,0:T(2,128)(2,1)S(1)}, u32[]{:S(2)}, u32[]{:S(2)}) async-start(bf16[32,2,2560]{2,1,0:T(2,128)(2,1)} %reshape.389), calls=%async_computation | async-start | bytes 655360 | tf_op jit(solution)/shard_map/while/body/eval_jaxpr/all_to_all | solution.py:98
  50.2 14.1 %all-to-all-start.1 = ((bf16[32,2,2560]{2,1,0:T(2,128)(2,1)}), bf16[32,2,2560]{2,1,0:T(2,128)(2,1)}, u32[]{:S(2)}, u32[]{:S(2)}) async-start(bf16[32,2,2560]{2,1,0:T(2,128)(2,1)} %reshape.392), calls=%async_computation.1 | async-start | bytes 655360 | tf_op jit(solution)/shard_map/while/body/eval_jaxpr/all_to_all | solution.py:100
  78.8 1.0 copy-start
  87.4 13.4 %all-to-all-start = ((bf16[32,2,2560]{2,1,0:T(2,128)(2,1)}), bf16[32,2,2560]{2,1,0:T(2,128)(2,1)S(1)}, u32[]{:S(2)}, u32[]{:S(2)}) async-start(bf16[32,2,2560]{2,1,0:T(2,128)(2,1)} %reshape.389), calls=%async_computation | async-start | bytes 655360 | tf_op jit(solution)/shard_map/while/body/eval_jaxpr/all_to_all | solution.py:98
  126.3 14.1 %all-to-all-start.1 = ((bf16[32,2,2560]{2,1,0:T(2,128)(2,1)}), bf16[32,2,2560]{2,1,0:T(2,128)(2,1)}, u32[]{:S(2)}, u32[]{:S(2)}) async-start(bf16[32,2,2560]{2,1,0:T(2,128)(2,1)} %reshape.392), calls=%async_computation.1 | async-start | bytes 655360 | tf_op jit(solution)/shard_map/while/body/eval_jaxpr/all_to_all | solution.py:100
  154.9 1.0 copy-start
  163.5 13.4 %all-to-all-start = ((bf16[32,2,2560]{2,1,0:T(2,128)(2,1)}), bf16[32,2,2560]{2,1,0:T(2,128)(2,1)S(1)}, u32[]{:S(2)}, u32[]{:S(2)}) async-start(bf16[32,2,2560]{2,1,0:T(2,128)(2,1)} %reshape.389), calls=%async_computation | async-start | bytes 655360 | tf_op jit(solution)/shard_map/while/body/eval_jaxpr/all_to_all | solution.py:98
  202.4 14.1 %all-to-all-start.1 = ((bf16[32,2,2560]{2,1,0:T(2,128)(2,1)}), bf16[32,2,2560]{2,1,0:T(2,128)(2,1)}, u32[]{:S(2)}, u32[]{:S(2)}) async-start(bf16[32,2,2560]{2,1,0:T(2,128)(2,1)} %reshape.392), calls=%async_computation.1 | async-start | bytes 655360 | tf_op jit(solution)/shard_map/while/body/eval_jaxpr/all_to_all | solution.py:100
  239.6 13.4 %all-to-all-start = ((bf16[32,2,2560]{2,1,0:T(2,128)(2,1)}), bf16[32,2,2560]{2,1,0:T(2,128)(2,1)S(1)}, u32[]{:S(2)}, u32[]{:S(2)}) async-start(bf16[32,2,2560]{2,1,0:T(2,128)(2,1)} %reshape.389), calls=%async_computation | async-start | bytes 655360 | tf_op jit(solution)/shard_map/while/body/eval_jaxpr/all_to_all | solution.py:98
  278.5 14.1 %all-to-all-start.1 = ((bf16[32,2,2560]{2,1,0:T(2,128)(2,1)}), bf16[32,2,2560]{2,1,0:T(2,128)(2,1)}, u32[]{:S(2)}, u32[]{:S(2)}) async-start(bf16[32,2,2560]{2,1,0:T(2,128)(2,1)} %reshape.392), calls=%async_computation.1 | async-start | bytes 655360 | tf_op jit(solution)/shard_map/while/body/eval_jaxpr/all_to_all | solution.py:100
  307.1 1.0 copy-start
  315.7 13.4 %all-to-all-start = ((bf16[32,2,2560]{2,1,0:T(2,128)(2,1)}), bf16[32,2,2560]{2,1,0:T(2,128)(2,1)S(1)}, u32[]{:S(2)}, u32[]{:S(2)}) async-start(bf16[32,2,2560]{2,1,0:T(2,128)(2,1)} %reshape.389), calls=%async_computation | async-start | bytes 655360 | tf_op jit(solution)/shard_map/while/body/eval_jaxpr/all_to_all | solution.py:98
  354.6 14.1 %all-to-all-start.1 = ((bf16[32,2,2560]{2,1,0:T(2,128)(2,1)}), bf16[32,2,2560]{2,1,0:T(2,128)(2,1)}, u32[]{:S(2)}, u32[]{:S(2)}) async-start(bf16[32,2,2560]{2,1,0:T(2,128)(2,1)} %reshape.392), calls=%async_computation.1 | async-start | bytes 655360 | tf_op jit(solution)/shard_map/while/body/eval_jaxpr/all_to_all | solution.py:100
  391.8 13.4 %all-to-all-start = ((bf16[32,2,2560]{2,1,0:T(2,128)(2,1)}), bf16[32,2,2560]{2,1,0:T(2,128)(2,1)S(1)}, u32[]{:S(2)}, u32[]{:S(2)}) async-start(bf16[32,2,2560]{2,1,0:T(2,128)(2,1)} %reshape.389), calls=%async_computation | async-start | bytes 655360 | tf_op jit(solution)/shard_map/while/body/eval_jaxpr/all_to_all | solution.py:98
  430.7 14.1 %all-to-all-start.1 = ((bf16[32,2,2560]{2,1,0:T(2,128)(2,1)}), bf16[32,2,2560]{2,1,0:T(2,128)(2,1)}, u32[]{:S(2)}, u32[]{:S(2)}) async-start(bf16[32,2,2560]{2,1,0:T(2,128)(2,1)} %reshape.392), calls=%async_computation.1 | async-start | bytes 655360 | tf_op jit(solution)/shard_map/while/body/eval_jaxpr/all_to_all | solution.py:100
  467.9 13.4 %all-to-all-start = ((bf16[32,2,2560]{2,1,0:T(2,128)(2,1)}), bf16[32,2,2560]{2,1,0:T(2,128)(2,1)S(1)}, u32[]{:S(2)}, u32[]{:S(2)}) async-start(bf16[32,2,2560]{2,1,0:T(2,128)(2,1)} %reshape.389), calls=%async_computation | async-start | bytes 655360 | tf_op jit(solution)/shard_map/while/body/eval_jaxpr/all_to_all | solution.py:98
  506.8 14.1 %all-to-all-start.1 = ((bf16[32,2,2560]{2,1,0:T(2,128)(2,1)}), bf16[32,2,2560]{2,1,0:T(2,128)(2,1)}, u32[]{:S(2)}, u32[]{:S(2)}) async-start(bf16[32,2,2560]{2,1,0:T(2,128)(2,1)} %reshape.392), calls=%async_computation.1 | async-start | bytes 655360 | tf_op jit(solution)/shard_map/while/body/eval_jaxpr/all_to_all | solution.py:100
  535.4 1.0 copy-start
  544.0 13.4 %all-to-all-start = ((bf16[32,2,2560]{2,1,0:T(2,128)(2,1)}), bf16[32,2,2560]{2,1,0:T(2,128)(2,1)S(1)}, u32[]{:S(2)}, u32[]{:S(2)}) async-start(bf16[32,2,2560]{2,1,0:T(2,128)(2,1)} %reshape.389), calls=%async_computation | async-start | bytes 655360 | tf_op jit(solution)/shard_map/while/body/eval_jaxpr/all_to_all | solution.py:98
  582.9 14.1 %all-to-all-start.1 = ((bf16[32,2,2560]{2,1,0:T(2,128)(2,1)}), bf16[32,2,2560]{2,1,0:T(2,128)(2,1)}, u32[]{:S(2)}, u32[]{:S(2)}) async-start(bf16[32,2,2560]{2,1,0:T(2,128)(2,1)} %reshape.392), calls=%async_computation.1 | async-start | bytes 655360 | tf_op jit(solution)/shard_map/while/body/eval_jaxpr/all_to_all | solution.py:100
  611.5 1.0 copy-start
  620.1 13.4 %all-to-all-start = ((bf16[32,2,2560]{2,1,0:T(2,128)(2,1)}), bf16[32,2,2560]{2,1,0:T(2,128)(2,1)S(1)}, u32[]{:S(2)}, u32[]{:S(2)}) async-start(bf16[32,2,2560]{2,1,0:T(2,128)(2,1)} %reshape.389), calls=%async_computation | async-start | bytes 655360 | tf_op jit(solution)/shard_map/while/body/eval_jaxpr/all_to_all | solution.py:98
  659.0 14.1 %all-to-all-start.1 = ((bf16[32,2,2560]{2,1,0:T(2,128)(2,1)}), bf16[32,2,2560]{2,1,0:T(2,128)(2,1)}, u32[]{:S(2)}, u32[]{:S(2)}) async-start(bf16[32,2,2560]{2,1,0:T(2,128)(2,1)} %reshape.392), calls=%async_computation.1 | async-start | bytes 655360 | tf_op jit(solution)/shard_map/while/body/eval_jaxpr/all_to_all | solution.py:100
  687.7 1.0 copy-start
  696.3 13.4 %all-to-all-start = ((bf16[32,2,2560]{2,1,0:T(2,128)(2,1)}), bf16[32,2,2560]{2,1,0:T(2,128)(2,1)S(1)}, u32[]{:S(2)}, u32[]{:S(2)}) async-start(bf16[32,2,2560]{2,1,0:T(2,128)(2,1)} %reshape.389), calls=%async_computation | async-start | bytes 655360 | tf_op jit(solution)/shard_map/while/body/eval_jaxpr/all_to_all | solution.py:98
  735.1 14.1 %all-to-all-start.1 = ((bf16[32,2,2560]{2,1,0:T(2,128)(2,1)}), bf16[32,2,2560]{2,1,0:T(2,128)(2,1)}, u32[]{:S(2)}, u32[]{:S(2)}) async-start(bf16[32,2,2560]{2,1,0:T(2,128)(2,1)} %reshape.392), calls=%async_computation.1 | async-start | bytes 655360 | tf_op jit(solution)/shard_map/while/body/eval_jaxpr/all_to_all | solution.py:100
  763.8 1.0 copy-start
  772.4 13.4 %all-to-all-start = ((bf16[32,2,2560]{2,1,0:T(2,128)(2,1)}), bf16[32,2,2560]{2,1,0:T(2,128)(2,1)S(1)}, u32[]{:S(2)}, u32[]{:S(2)}) async-start(bf16[32,2,2560]{2,1,0:T(2,128)(2,1)} %reshape.389), calls=%async_computation | async-start | bytes 655360 | tf_op jit(solution)/shard_map/while/body/eval_jaxpr/all_to_all | solution.py:98
  811.2 14.1 %all-to-all-start.1 = ((bf16[32,2,2560]{2,1,0:T(2,128)(2,1)}), bf16[32,2,2560]{2,1,0:T(2,128)(2,1)}, u32[]{:S(2)}, u32[]{:S(2)}) async-start(bf16[32,2,2560]{2,1,0:T(2,128)(2,1)} %reshape.392), calls=%async_computation.1 | async-start | bytes 655360 | tf_op jit(solution)/shard_map/while/body/eval_jaxpr/all_to_all | solution.py:100
  848.5 13.4 %all-to-all-start = ((bf16[32,2,2560]{2,1,0:T(2,128)(2,1)}), bf16[32,2,2560]{2,1,0:T(2,128)(2,1)S(1)}, u32[]{:S(2)}, u32[]{:S(2)}) async-start(bf16[32,2,2560]{2,1,0:T(2,128)(2,1)} %reshape.389), calls=%async_computation | async-start | bytes 655360 | tf_op jit(solution)/shard_map/while/body/eval_jaxpr/all_to_all | solution.py:98
  887.3 14.1 %all-to-all-start.1 = ((bf16[32,2,2560]{2,1,0:T(2,128)(2,1)}), bf16[32,2,2560]{2,1,0:T(2,128)(2,1)}, u32[]{:S(2)}, u32[]{:S(2)}) async-start(bf16[32,2,2560]{2,1,0:T(2,128)(2,1)} %reshape.392), calls=%async_computation.1 | async-start | bytes 655360 | tf_op jit(solution)/shard_map/while/body/eval_jaxpr/all_to_all | solution.py:100
  921.0 9.4 copy-start.7
  921.1 12.2 %collective-permute-start = (bf16[12,1,8,256]{3,2,0,1:T(8,128)(2,1)S(1)}, bf16[12,1,8,256]{3,2,0,1:T(8,128)(2,1)S(1)}, u32[]{:S(2)}, u32[]{:S(2)}) collective-permute-start(bf16[12,1,8,256]{3,2,0,1:T(8,128)(2,1)S(1)} %get-tuple-element.349), channel_id=1, source_target_pairs={{0,4},{4,8},{8,12},{12,16},{16,20},{20,24},{24,28},{28,32},{32,36}... | collective-permute-start | bytes 147464 | tf_op jit(solution)/shard_map/ppermute | solution.py:22
  924.3 9.0 collective-permute-start.1
  932.0 2.2 copy-start.2
  932.0 2.2 copy-start.3
  932.0 2.2 copy-start.11
  1103.9 50.1 %copy-start.1 = (f32[1,32,1440]{2,1,0:T(8,128)}, f32[1,32,1440]{2,1,0:T(8,128)S(1)}, u32[]{:S(2)}) copy-start(f32[1,32,1440]{2,1,0:T(8,128)S(1)} %get-tuple-element.305) | copy-start | bytes 552964
  1103.9 41.8 %copy-start.13 = (f32[40]{0:T(128)S(1)}, f32[40]{0:T(128)}, u32[]{:S(2)}) copy-start(f32[40]{0:T(128)} %param.35) | copy-start | bytes 484
  1104.4 42.0 %collective-permute-start.2 = (bf16[12,1,32,256]{3,2,0,1:T(8,128)(2,1)S(1)}, bf16[12,1,32,256]{3,2,0,1:T(8,128)(2,1)S(1)}, u32[]{:S(2)}, u32[]{:S(2)}) collective-permute-start(bf16[12,1,32,256]{3,2,0,1:T(8,128)(2,1)S(1)} %fusion.46), channel_id=1, source_target_pairs={{0,4},{4,8},{8,12},{12,16},{16,20},{20,24},{24,28},{28,32},{32,36}... | collective-permute-start | bytes 589832 | tf_op jit(solution)/shard_map/ppermute | solution.py:22
  1143.8 9.1 collective-permute-start.3
  (5 other events, 4.9 us)
where the time goes:
time: 1160 us; the launch traced here: 1150 us
  local copies, waits for them, and re-layouts  398 us (34%)
  matrix products  238 us (21%)
  starting transfers between devices  181 us (16%)
  waiting for transfers between devices  180 us (16%)
  blocking collectives  119 us (10%)
  other arithmetic  34.7 us (3%)
    dot_general x12, matrix products, padded_transform(): jnp.einsum('rmnc,mln->rlmc', damped, tables, preferred_element_type=jnp.f...  182 us
    while x84, local copies, waits for them, and re-layouts  153 us
    all_gather x12, blocking collectives, ocean_advance(): lax.all_gather(ocean_now.astype(jnp.bfloat16), 'lev', axis=0, tiled=True)  119 us
    convert_element_type x36, local copies, waits for them, and re-layouts, march_air_model(): synthesis_field = returned.reshape(field_local, height_pile, lat_local, c...  108 us
    all_to_all x12, waiting for transfers between devices, march_air_model(): lax.all_to_all(scaled, 'band', split_axis=2, concat_axis=1, tiled=True)  97.5 us
    all_to_all x12, waiting for transfers between devices, march_air_model(): lax.all_to_all(synthesis, 'band', split_axis=1, concat_axis=2, tiled=True)  74.9 us
    all_to_all x12, starting transfers between devices, march_air_model(): lax.all_to_all(synthesis, 'band', split_axis=1, concat_axis=2, tiled=True)  69.3 us
    all_to_all x12, starting transfers between devices, march_air_model(): lax.all_to_all(scaled, 'band', split_axis=2, concat_axis=1, tiled=True)  65.2 us
  transfers between devices with their start and end apart: 28, of which 26 were waited for; matrix products, arithmetic and copies ran while one was open for 3% of the time, Pallas kernels for 0%

commit v1 on v0

--- a/solution.py
+++ b/solution.py
@@ -97,7 +97,12 @@
         scaled = scaled.reshape(row_count, lat_local, column_count)
         by_wave = lax.all_to_all(scaled, "band", split_axis=2, concat_axis=1, tiled=True)
         synthesis = transform(by_wave)
-        returned = lax.all_to_all(synthesis, "band", split_axis=1, concat_axis=2, tiled=True)
+        returned = jnp.concatenate(
+            lax.all_to_all(
+                jnp.stack(jnp.split(synthesis, lax.axis_size("band"), axis=1)), "band", 0, 0
+            ),
+            axis=2,
+        )
         synthesis_field = returned.reshape(
             field_local, height_pile, lat_local, column_count
         ).astype(jnp.float32)

time: 1160 us -> 1000 us (0.86)
  local copies, waits for them, and re-layouts: 398 us -> 238 us
  matrix products: 238 us -> 220 us
  other arithmetic: 34.7 us -> 49.4 us
    convert_element_type x36 -> x12, local copies, waits for them, and re-layouts: 108 us -> 22.5 us  [march_air_model(): synthesis_field = returned.reshape(field_local, height_pile, lat_local, c...]
    reshape x12 -> x0, local copies, waits for them, and re-layouts: 31.7 us -> none  [padded_transform(): synthesis.astype(jnp.bfloat16).reshape(row_count, lat_count, wave_count * 2)]
    while x84 -> x480, local copies, waits for them, and re-layouts: 153 us -> 125 us
    all_to_all x12 -> x0, local copies, waits for them, and re-layouts: 28.3 us -> none  [march_air_model(): lax.all_to_all(synthesis, 'band', split_axis=1, concat_axis=2, tiled=True)]
    sub x12, other arithmetic: 10.8 us -> 23.9 us  [march_air_model(): halfway_point = air_model_present - synthesis_field]
  transfers between devices with their start and end apart: 28 -> 28, of which waited for: 26 -> 26; matrix products, arithmetic and copies ran while one was open for 3% -> 2% of each run, Pallas kernels for 0% -> 0%
where the time goes in v1:
time: 1000 us; the launch traced here: 996 us
  local copies, waits for them, and re-layouts  238 us (24%)
  matrix products  220 us (22%)
  waiting for transfers between devices  191 us (19%)
  starting transfers between devices  172 us (17%)
  blocking collectives  121 us (12%)
  other arithmetic  49.4 us (5%)
    dot_general x12, matrix products, padded_transform(): jnp.einsum('rmnc,mln->rlmc', damped, tables, preferred_element_type=jnp.f...  173 us
    while x480, local copies, waits for them, and re-layouts  125 us
    all_gather x12, blocking collectives, ocean_advance(): lax.all_gather(ocean_now.astype(jnp.bfloat16), 'lev', axis=0, tiled=True)  121 us
    all_to_all x12, waiting for transfers between devices, march_air_model(): lax.all_to_all(scaled, 'band', split_axis=2, concat_axis=1, tiled=True)  97.5 us
    all_to_all x12, waiting for transfers between devices, march_air_model(): lax.all_to_all(jnp.stack(jnp.split(synthesis, lax.axis_size('band'), axis...  86.5 us
    all_to_all x12, starting transfers between devices, march_air_model(): lax.all_to_all(scaled, 'band', split_axis=2, concat_axis=1, tiled=True)  65.2 us
    all_to_all x12, starting transfers between devices, march_air_model(): lax.all_to_all(jnp.stack(jnp.split(synthesis, lax.axis_size('band'), axis...  61.6 us
    ppermute x2, starting transfers between devices, with_halo(): before = lax.ppermute(last, axis, up)  41.3 us
  transfers between devices with their start and end apart: 28, of which 26 were waited for; matrix products, arithmetic and copies ran while one was open for 2% of the time, Pallas kernels for 0%

profile of v1, /device:TPU:15, one launch (start us, length us, event | category | flops | bytes accessed | tf_op | source)
XLA Modules:
  0.0 996.5 jit_solution(5319033591037402079)
XLA Ops:
  4.0 767.4 %while.29 = (s32[]{:T(128)}, f32[1,16,40,256]{3,1,2,0:T(8,128)S(1)}, bf16[12,1,40,256]{3,2,1,0:T(8,128)(2,1)}, f32[40]{0:T(128)S(1)}, bf16[4,1280,1280]{2,1,0:T(...) while((s32[]{:T(128)}, ...), condition=%wide.region_1.2_spmd.clone, body=%wide.region_0.1_spmd.clone.sunk | while | flops 871715840 | bytes 35641944 | solution.py:119
  8.5 8.7 all-to-all-start
  17.3 8.1 all-to-all-done
  29.6 14.4 %fusion.114 = bf16[4,16,2,1280]{3,1,2,0:T(8,128)(2,1)S(1)} fusion(bf16[4,1280,1280]{2,1,0:T(8,128)(2,1)} %get-tuple-element.557, bf16[16,1280,4,2]{1,0,3,2:T(8,128)(2,1)S(1)} %reshape.389, f32[4,1280]{1,0:T(4,128)S(1)} %divide_select_fusion.2), kind=kOutput, calls=%fused_computation.17.clone.1 | convolution fusion | flops 839516160 | bytes 13783040 | tf_op jit(solution)/shard_map/while/body/eval_jaxpr/rmnc,mln->rlmc/dot_general | solution.py:50
  53.7 7.2 all-to-all-done.1
  80.9 8.1 all-to-all-done
  93.2 14.4 %fusion.114 = bf16[4,16,2,1280]{3,1,2,0:T(8,128)(2,1)S(1)} fusion(bf16[4,1280,1280]{2,1,0:T(8,128)(2,1)} %get-tuple-element.557, bf16[16,1280,4,2]{1,0,3,2:T(8,128)(2,1)S(1)} %reshape.389, f32[4,1280]{1,0:T(4,128)S(1)} %divide_select_fusion.2), kind=kOutput, calls=%fused_computation.17.clone.1 | convolution fusion | flops 839516160 | bytes 13783040 | tf_op jit(solution)/shard_map/while/body/eval_jaxpr/rmnc,mln->rlmc/dot_general | solution.py:50
  117.4 7.2 all-to-all-done.1
  144.5 8.1 all-to-all-done
  156.9 14.4 %fusion.114 = bf16[4,16,2,1280]{3,1,2,0:T(8,128)(2,1)S(1)} fusion(bf16[4,1280,1280]{2,1,0:T(8,128)(2,1)} %get-tuple-element.557, bf16[16,1280,4,2]{1,0,3,2:T(8,128)(2,1)S(1)} %reshape.389, f32[4,1280]{1,0:T(4,128)S(1)} %divide_select_fusion.2), kind=kOutput, calls=%fused_computation.17.clone.1 | convolution fusion | flops 839516160 | bytes 13783040 | tf_op jit(solution)/shard_map/while/body/eval_jaxpr/rmnc,mln->rlmc/dot_general | solution.py:50
  181.0 7.2 all-to-all-done.1
  208.2 8.1 all-to-all-done
  220.5 14.4 %fusion.114 = bf16[4,16,2,1280]{3,1,2,0:T(8,128)(2,1)S(1)} fusion(bf16[4,1280,1280]{2,1,0:T(8,128)(2,1)} %get-tuple-element.557, bf16[16,1280,4,2]{1,0,3,2:T(8,128)(2,1)S(1)} %reshape.389, f32[4,1280]{1,0:T(4,128)S(1)} %divide_select_fusion.2), kind=kOutput, calls=%fused_computation.17.clone.1 | convolution fusion | flops 839516160 | bytes 13783040 | tf_op jit(solution)/shard_map/while/body/eval_jaxpr/rmnc,mln->rlmc/dot_general | solution.py:50
  244.6 7.2 all-to-all-done.1
  271.8 8.1 all-to-all-done
  284.1 14.4 %fusion.114 = bf16[4,16,2,1280]{3,1,2,0:T(8,128)(2,1)S(1)} fusion(bf16[4,1280,1280]{2,1,0:T(8,128)(2,1)} %get-tuple-element.557, bf16[16,1280,4,2]{1,0,3,2:T(8,128)(2,1)S(1)} %reshape.389, f32[4,1280]{1,0:T(4,128)S(1)} %divide_select_fusion.2), kind=kOutput, calls=%fused_computation.17.clone.1 | convolution fusion | flops 839516160 | bytes 13783040 | tf_op jit(solution)/shard_map/while/body/eval_jaxpr/rmnc,mln->rlmc/dot_general | solution.py:50
  308.3 7.2 all-to-all-done.1
  335.5 8.1 all-to-all-done
  347.8 14.4 %fusion.114 = bf16[4,16,2,1280]{3,1,2,0:T(8,128)(2,1)S(1)} fusion(bf16[4,1280,1280]{2,1,0:T(8,128)(2,1)} %get-tuple-element.557, bf16[16,1280,4,2]{1,0,3,2:T(8,128)(2,1)S(1)} %reshape.389, f32[4,1280]{1,0:T(4,128)S(1)} %divide_select_fusion.2), kind=kOutput, calls=%fused_computation.17.clone.1 | convolution fusion | flops 839516160 | bytes 13783040 | tf_op jit(solution)/shard_map/while/body/eval_jaxpr/rmnc,mln->rlmc/dot_general | solution.py:50
  371.9 7.2 all-to-all-done.1
  399.1 8.1 all-to-all-done
  411.4 14.4 %fusion.114 = bf16[4,16,2,1280]{3,1,2,0:T(8,128)(2,1)S(1)} fusion(bf16[4,1280,1280]{2,1,0:T(8,128)(2,1)} %get-tuple-element.557, bf16[16,1280,4,2]{1,0,3,2:T(8,128)(2,1)S(1)} %reshape.389, f32[4,1280]{1,0:T(4,128)S(1)} %divide_select_fusion.2), kind=kOutput, calls=%fused_computation.17.clone.1 | convolution fusion | flops 839516160 | bytes 13783040 | tf_op jit(solution)/shard_map/while/body/eval_jaxpr/rmnc,mln->rlmc/dot_general | solution.py:50
  435.6 7.2 all-to-all-done.1
  462.7 8.1 all-to-all-done
  475.1 14.4 %fusion.114 = bf16[4,16,2,1280]{3,1,2,0:T(8,128)(2,1)S(1)} fusion(bf16[4,1280,1280]{2,1,0:T(8,128)(2,1)} %get-tuple-element.557, bf16[16,1280,4,2]{1,0,3,2:T(8,128)(2,1)S(1)} %reshape.389, f32[4,1280]{1,0:T(4,128)S(1)} %divide_select_fusion.2), kind=kOutput, calls=%fused_computation.17.clone.1 | convolution fusion | flops 839516160 | bytes 13783040 | tf_op jit(solution)/shard_map/while/body/eval_jaxpr/rmnc,mln->rlmc/dot_general | solution.py:50
  499.2 7.2 all-to-all-done.1
  526.4 8.1 all-to-all-done
  538.7 14.4 %fusion.114 = bf16[4,16,2,1280]{3,1,2,0:T(8,128)(2,1)S(1)} fusion(bf16[4,1280,1280]{2,1,0:T(8,128)(2,1)} %get-tuple-element.557, bf16[16,1280,4,2]{1,0,3,2:T(8,128)(2,1)S(1)} %reshape.389, f32[4,1280]{1,0:T(4,128)S(1)} %divide_select_fusion.2), kind=kOutput, calls=%fused_computation.17.clone.1 | convolution fusion | flops 839516160 | bytes 13783040 | tf_op jit(solution)/shard_map/while/body/eval_jaxpr/rmnc,mln->rlmc/dot_general | solution.py:50
  590.0 8.1 all-to-all-done
  602.4 14.4 %fusion.114 = bf16[4,16,2,1280]{3,1,2,0:T(8,128)(2,1)S(1)} fusion(bf16[4,1280,1280]{2,1,0:T(8,128)(2,1)} %get-tuple-element.557, bf16[16,1280,4,2]{1,0,3,2:T(8,128)(2,1)S(1)} %reshape.389, f32[4,1280]{1,0:T(4,128)S(1)} %divide_select_fusion.2), kind=kOutput, calls=%fused_computation.17.clone.1 | convolution fusion | flops 839516160 | bytes 13783040 | tf_op jit(solution)/shard_map/while/body/eval_jaxpr/rmnc,mln->rlmc/dot_general | solution.py:50
  653.7 8.1 all-to-all-done
  666.0 14.4 %fusion.114 = bf16[4,16,2,1280]{3,1,2,0:T(8,128)(2,1)S(1)} fusion(bf16[4,1280,1280]{2,1,0:T(8,128)(2,1)} %get-tuple-element.557, bf16[16,1280,4,2]{1,0,3,2:T(8,128)(2,1)S(1)} %reshape.389, f32[4,1280]{1,0:T(4,128)S(1)} %divide_select_fusion.2), kind=kOutput, calls=%fused_computation.17.clone.1 | convolution fusion | flops 839516160 | bytes 13783040 | tf_op jit(solution)/shard_map/while/body/eval_jaxpr/rmnc,mln->rlmc/dot_general | solution.py:50
  717.3 8.1 all-to-all-done
  729.6 14.4 %fusion.114 = bf16[4,16,2,1280]{3,1,2,0:T(8,128)(2,1)S(1)} fusion(bf16[4,1280,1280]{2,1,0:T(8,128)(2,1)} %get-tuple-element.557, bf16[16,1280,4,2]{1,0,3,2:T(8,128)(2,1)S(1)} %reshape.389, f32[4,1280]{1,0:T(4,128)S(1)} %divide_select_fusion.2), kind=kOutput, calls=%fused_computation.17.clone.1 | convolution fusion | flops 839516160 | bytes 13783040 | tf_op jit(solution)/shard_map/while/body/eval_jaxpr/rmnc,mln->rlmc/dot_general | solution.py:50
  784.7 162.9 %while.28 = (s32[]{:T(128)}, f32[1,32,1440]{2,1,0:T(8,128)S(1)}, bf16[12,1,32,1440]{3,2,1,0:T(8,128)(2,1)S(1)}, f32[1,4]{1,0:T(1,128)S(1)}, bf16[12,1,32,256]{3,...) while((s32[]{:T(128)}, f32[1,32,1440]{2,1,0:T(8,128)S(1)}, ...), condition=%wide.region_3.4_spmd, body=%wide.region_2.3_spmd.sunk | while | flops 24514560 | bytes 2624629 | solution.py:166
  785.4 9.9 all_gather.4
  798.8 10.5 %all_gather.4 = bf16[4,32,1440]{2,1,0:T(8,128)(2,1)S(1)} all-gather(bf16[1,32,1440]{2,1,0:T(8,128)(2,1)S(1)} %convert_element_type.205), channel_id=1, replica_groups=mesh['band'=32,'lev'=4] {'lev'}, dimensions={0}, use_global_device_ids=true | all-gather | bytes 460800 | tf_op jit(solution)/shard_map/while/body/eval_jaxpr/all_gather | solution.py:153
  812.8 9.3 all_gather.4
  825.7 10.2 %all_gather.4 = bf16[4,32,1440]{2,1,0:T(8,128)(2,1)S(1)} all-gather(bf16[1,32,1440]{2,1,0:T(8,128)(2,1)S(1)} %convert_element_type.205), channel_id=1, replica_groups=mesh['band'=32,'lev'=4] {'lev'}, dimensions={0}, use_global_device_ids=true | all-gather | bytes 460800 | tf_op jit(solution)/shard_map/while/body/eval_jaxpr/all_gather | solution.py:153
  839.4 9.6 all_gather.4
  852.5 10.9 %all_gather.4 = bf16[4,32,1440]{2,1,0:T(8,128)(2,1)S(1)} all-gather(bf16[1,32,1440]{2,1,0:T(8,128)(2,1)S(1)} %convert_element_type.205), channel_id=1, replica_groups=mesh['band'=32,'lev'=4] {'lev'}, dimensions={0}, use_global_device_ids=true | all-gather | bytes 460800 | tf_op jit(solution)/shard_map/while/body/eval_jaxpr/all_gather | solution.py:153
  866.9 9.6 all_gather.4
  880.1 10.5 %all_gather.4 = bf16[4,32,1440]{2,1,0:T(8,128)(2,1)S(1)} all-gather(bf16[1,32,1440]{2,1,0:T(8,128)(2,1)S(1)} %convert_element_type.205), channel_id=1, replica_groups=mesh['band'=32,'lev'=4] {'lev'}, dimensions={0}, use_global_device_ids=true | all-gather | bytes 460800 | tf_op jit(solution)/shard_map/while/body/eval_jaxpr/all_gather | solution.py:153
  894.1 9.3 all_gather.4
  906.9 10.4 %all_gather.4 = bf16[4,32,1440]{2,1,0:T(8,128)(2,1)S(1)} all-gather(bf16[1,32,1440]{2,1,0:T(8,128)(2,1)S(1)} %convert_element_type.205), channel_id=1, replica_groups=mesh['band'=32,'lev'=4] {'lev'}, dimensions={0}, use_global_device_ids=true | all-gather | bytes 460800 | tf_op jit(solution)/shard_map/while/body/eval_jaxpr/all_gather | solution.py:153
  920.8 9.6 all_gather.4
  934.0 10.8 %all_gather.4 = bf16[4,32,1440]{2,1,0:T(8,128)(2,1)S(1)} all-gather(bf16[1,32,1440]{2,1,0:T(8,128)(2,1)S(1)} %convert_element_type.205), channel_id=1, replica_groups=mesh['band'=32,'lev'=4] {'lev'}, dimensions={0}, use_global_device_ids=true | all-gather | bytes 460800 | tf_op jit(solution)/shard_map/while/body/eval_jaxpr/all_gather | solution.py:153
  948.2 38.1 %collective-permute-start.2 = (bf16[12,1,32,256]{3,2,0,1:T(8,128)(2,1)S(1)}, bf16[12,1,32,256]{3,2,0,1:T(8,128)(2,1)S(1)}, u32[]{:S(2)}, u32[]{:S(2)}) collective-permute-start(bf16[12,1,32,256]{3,2,0,1:T(8,128)(2,1)S(1)} %fusion.46), channel_id=1, source_target_pairs={{0,4},{4,8},{8,12},{12,16},{16,20},{20,24},{24,28},{28,32},{32,36}... | collective-permute-start | bytes 589832 | tf_op jit(solution)/shard_map/ppermute | solution.py:22
  (797 shorter events, 494.5 us)
Async XLA Ops:
  0.6 2.6 copy-start.15
  0.7 2.6 copy-start.11
  4.0 777.3 %copy-start.9 = (f32[4,4]{1,0:T(4,128)S(1)}, f32[4,4]{1,0:T(4,128)}, u32[]{:S(2)}) copy-start(f32[4,4]{1,0:T(4,128)} %param.30) | copy-start | bytes 196
  4.0 777.4 %copy-start.12 = (s32[32]{0:T(128)S(1)}, s32[32]{0:T(128)}, u32[]{:S(2)}) copy-start(s32[32]{0:T(128)} %param.32) | copy-start | bytes 388
  4.0 777.4 %copy-start.13 = (f32[32]{0:T(128)S(1)}, f32[32]{0:T(128)}, u32[]{:S(2)}) copy-start(f32[32]{0:T(128)} %param.33) | copy-start | bytes 388
  8.5 16.8 %all-to-all-start = ((bf16[32,2,2560]{2,1,0:T(2,128)(2,1)}), bf16[32,2,2560]{2,1,0:T(2,128)(2,1)S(1)}, u32[]{:S(2)}, u32[]{:S(2)}) async-start(bf16[32,2,2560]{2,1,0:T(2,128)(2,1)} %reshape.387), calls=%async_computation | async-start | bytes 655360 | tf_op jit(solution)/shard_map/while/body/eval_jaxpr/all_to_all | solution.py:98
  47.6 13.4 %all-to-all-start.1 = ((bf16[32,2,2560]{2,1,0:T(2,128)(2,1)}), bf16[32,2,2560]{2,1,0:T(2,128)(2,1)S(1)}, u32[]{:S(2)}, u32[]{:S(2)}) async-start(bf16[32,2,2560]{2,1,0:T(2,128)(2,1)} %reshape.390), calls=%async_computation.1 | async-start | bytes 655360 | tf_op jit(solution)/shard_map/while/body/eval_jaxpr/all_to_all | solution.py:101
  66.6 4.5 copy-start.2
  75.7 13.4 %all-to-all-start = ((bf16[32,2,2560]{2,1,0:T(2,128)(2,1)}), bf16[32,2,2560]{2,1,0:T(2,128)(2,1)S(1)}, u32[]{:S(2)}, u32[]{:S(2)}) async-start(bf16[32,2,2560]{2,1,0:T(2,128)(2,1)} %reshape.387), calls=%async_computation | async-start | bytes 655360 | tf_op jit(solution)/shard_map/while/body/eval_jaxpr/all_to_all | solution.py:98
  111.2 13.4 %all-to-all-start.1 = ((bf16[32,2,2560]{2,1,0:T(2,128)(2,1)}), bf16[32,2,2560]{2,1,0:T(2,128)(2,1)S(1)}, u32[]{:S(2)}, u32[]{:S(2)}) async-start(bf16[32,2,2560]{2,1,0:T(2,128)(2,1)} %reshape.390), calls=%async_computation.1 | async-start | bytes 655360 | tf_op jit(solution)/shard_map/while/body/eval_jaxpr/all_to_all | solution.py:101
  130.3 4.5 copy-start.2
  139.3 13.4 %all-to-all-start = ((bf16[32,2,2560]{2,1,0:T(2,128)(2,1)}), bf16[32,2,2560]{2,1,0:T(2,128)(2,1)S(1)}, u32[]{:S(2)}, u32[]{:S(2)}) async-start(bf16[32,2,2560]{2,1,0:T(2,128)(2,1)} %reshape.387), calls=%async_computation | async-start | bytes 655360 | tf_op jit(solution)/shard_map/while/body/eval_jaxpr/all_to_all | solution.py:98
  174.8 13.4 %all-to-all-start.1 = ((bf16[32,2,2560]{2,1,0:T(2,128)(2,1)}), bf16[32,2,2560]{2,1,0:T(2,128)(2,1)S(1)}, u32[]{:S(2)}, u32[]{:S(2)}) async-start(bf16[32,2,2560]{2,1,0:T(2,128)(2,1)} %reshape.390), calls=%async_computation.1 | async-start | bytes 655360 | tf_op jit(solution)/shard_map/while/body/eval_jaxpr/all_to_all | solution.py:101
  193.9 4.5 copy-start.2
  202.9 13.4 %all-to-all-start = ((bf16[32,2,2560]{2,1,0:T(2,128)(2,1)}), bf16[32,2,2560]{2,1,0:T(2,128)(2,1)S(1)}, u32[]{:S(2)}, u32[]{:S(2)}) async-start(bf16[32,2,2560]{2,1,0:T(2,128)(2,1)} %reshape.387), calls=%async_computation | async-start | bytes 655360 | tf_op jit(solution)/shard_map/while/body/eval_jaxpr/all_to_all | solution.py:98
  238.5 13.4 %all-to-all-start.1 = ((bf16[32,2,2560]{2,1,0:T(2,128)(2,1)}), bf16[32,2,2560]{2,1,0:T(2,128)(2,1)S(1)}, u32[]{:S(2)}, u32[]{:S(2)}) async-start(bf16[32,2,2560]{2,1,0:T(2,128)(2,1)} %reshape.390), calls=%async_computation.1 | async-start | bytes 655360 | tf_op jit(solution)/shard_map/while/body/eval_jaxpr/all_to_all | solution.py:101
  257.6 4.5 copy-start.2
  266.6 13.4 %all-to-all-start = ((bf16[32,2,2560]{2,1,0:T(2,128)(2,1)}), bf16[32,2,2560]{2,1,0:T(2,128)(2,1)S(1)}, u32[]{:S(2)}, u32[]{:S(2)}) async-start(bf16[32,2,2560]{2,1,0:T(2,128)(2,1)} %reshape.387), calls=%async_computation | async-start | bytes 655360 | tf_op jit(solution)/shard_map/while/body/eval_jaxpr/all_to_all | solution.py:98
  302.1 13.4 %all-to-all-start.1 = ((bf16[32,2,2560]{2,1,0:T(2,128)(2,1)}), bf16[32,2,2560]{2,1,0:T(2,128)(2,1)S(1)}, u32[]{:S(2)}, u32[]{:S(2)}) async-start(bf16[32,2,2560]{2,1,0:T(2,128)(2,1)} %reshape.390), calls=%async_computation.1 | async-start | bytes 655360 | tf_op jit(solution)/shard_map/while/body/eval_jaxpr/all_to_all | solution.py:101
  321.2 4.5 copy-start.2
  330.2 13.4 %all-to-all-start = ((bf16[32,2,2560]{2,1,0:T(2,128)(2,1)}), bf16[32,2,2560]{2,1,0:T(2,128)(2,1)S(1)}, u32[]{:S(2)}, u32[]{:S(2)}) async-start(bf16[32,2,2560]{2,1,0:T(2,128)(2,1)} %reshape.387), calls=%async_computation | async-start | bytes 655360 | tf_op jit(solution)/shard_map/while/body/eval_jaxpr/all_to_all | solution.py:98
  365.8 13.4 %all-to-all-start.1 = ((bf16[32,2,2560]{2,1,0:T(2,128)(2,1)}), bf16[32,2,2560]{2,1,0:T(2,128)(2,1)S(1)}, u32[]{:S(2)}, u32[]{:S(2)}) async-start(bf16[32,2,2560]{2,1,0:T(2,128)(2,1)} %reshape.390), calls=%async_computation.1 | async-start | bytes 655360 | tf_op jit(solution)/shard_map/while/body/eval_jaxpr/all_to_all | solution.py:101
  384.9 4.5 copy-start.2
  393.9 13.4 %all-to-all-start = ((bf16[32,2,2560]{2,1,0:T(2,128)(2,1)}), bf16[32,2,2560]{2,1,0:T(2,128)(2,1)S(1)}, u32[]{:S(2)}, u32[]{:S(2)}) async-start(bf16[32,2,2560]{2,1,0:T(2,128)(2,1)} %reshape.387), calls=%async_computation | async-start | bytes 655360 | tf_op jit(solution)/shard_map/while/body/eval_jaxpr/all_to_all | solution.py:98
  429.4 13.4 %all-to-all-start.1 = ((bf16[32,2,2560]{2,1,0:T(2,128)(2,1)}), bf16[32,2,2560]{2,1,0:T(2,128)(2,1)S(1)}, u32[]{:S(2)}, u32[]{:S(2)}) async-start(bf16[32,2,2560]{2,1,0:T(2,128)(2,1)} %reshape.390), calls=%async_computation.1 | async-start | bytes 655360 | tf_op jit(solution)/shard_map/while/body/eval_jaxpr/all_to_all | solution.py:101
  448.5 4.5 copy-start.2
  457.5 13.4 %all-to-all-start = ((bf16[32,2,2560]{2,1,0:T(2,128)(2,1)}), bf16[32,2,2560]{2,1,0:T(2,128)(2,1)S(1)}, u32[]{:S(2)}, u32[]{:S(2)}) async-start(bf16[32,2,2560]{2,1,0:T(2,128)(2,1)} %reshape.387), calls=%async_computation | async-start | bytes 655360 | tf_op jit(solution)/shard_map/while/body/eval_jaxpr/all_to_all | solution.py:98
  493.0 13.4 %all-to-all-start.1 = ((bf16[32,2,2560]{2,1,0:T(2,128)(2,1)}), bf16[32,2,2560]{2,1,0:T(2,128)(2,1)S(1)}, u32[]{:S(2)}, u32[]{:S(2)}) async-start(bf16[32,2,2560]{2,1,0:T(2,128)(2,1)} %reshape.390), calls=%async_computation.1 | async-start | bytes 655360 | tf_op jit(solution)/shard_map/while/body/eval_jaxpr/all_to_all | solution.py:101
  512.1 4.5 copy-start.2
  521.2 13.4 %all-to-all-start = ((bf16[32,2,2560]{2,1,0:T(2,128)(2,1)}), bf16[32,2,2560]{2,1,0:T(2,128)(2,1)S(1)}, u32[]{:S(2)}, u32[]{:S(2)}) async-start(bf16[32,2,2560]{2,1,0:T(2,128)(2,1)} %reshape.387), calls=%async_computation | async-start | bytes 655360 | tf_op jit(solution)/shard_map/while/body/eval_jaxpr/all_to_all | solution.py:98
  556.7 13.4 %all-to-all-start.1 = ((bf16[32,2,2560]{2,1,0:T(2,128)(2,1)}), bf16[32,2,2560]{2,1,0:T(2,128)(2,1)S(1)}, u32[]{:S(2)}, u32[]{:S(2)}) async-start(bf16[32,2,2560]{2,1,0:T(2,128)(2,1)} %reshape.390), calls=%async_computation.1 | async-start | bytes 655360 | tf_op jit(solution)/shard_map/while/body/eval_jaxpr/all_to_all | solution.py:101
  575.8 4.5 copy-start.2
  584.8 13.4 %all-to-all-start = ((bf16[32,2,2560]{2,1,0:T(2,128)(2,1)}), bf16[32,2,2560]{2,1,0:T(2,128)(2,1)S(1)}, u32[]{:S(2)}, u32[]{:S(2)}) async-start(bf16[32,2,2560]{2,1,0:T(2,128)(2,1)} %reshape.387), calls=%async_computation | async-start | bytes 655360 | tf_op jit(solution)/shard_map/while/body/eval_jaxpr/all_to_all | solution.py:98
  620.3 13.4 %all-to-all-start.1 = ((bf16[32,2,2560]{2,1,0:T(2,128)(2,1)}), bf16[32,2,2560]{2,1,0:T(2,128)(2,1)S(1)}, u32[]{:S(2)}, u32[]{:S(2)}) async-start(bf16[32,2,2560]{2,1,0:T(2,128)(2,1)} %reshape.390), calls=%async_computation.1 | async-start | bytes 655360 | tf_op jit(solution)/shard_map/while/body/eval_jaxpr/all_to_all | solution.py:101
  639.4 4.4 copy-start.2
  648.4 13.4 %all-to-all-start = ((bf16[32,2,2560]{2,1,0:T(2,128)(2,1)}), bf16[32,2,2560]{2,1,0:T(2,128)(2,1)S(1)}, u32[]{:S(2)}, u32[]{:S(2)}) async-start(bf16[32,2,2560]{2,1,0:T(2,128)(2,1)} %reshape.387), calls=%async_computation | async-start | bytes 655360 | tf_op jit(solution)/shard_map/while/body/eval_jaxpr/all_to_all | solution.py:98
  684.0 13.4 %all-to-all-start.1 = ((bf16[32,2,2560]{2,1,0:T(2,128)(2,1)}), bf16[32,2,2560]{2,1,0:T(2,128)(2,1)S(1)}, u32[]{:S(2)}, u32[]{:S(2)}) async-start(bf16[32,2,2560]{2,1,0:T(2,128)(2,1)} %reshape.390), calls=%async_computation.1 | async-start | bytes 655360 | tf_op jit(solution)/shard_map/while/body/eval_jaxpr/all_to_all | solution.py:101
  703.1 4.5 copy-start.2
  712.1 13.4 %all-to-all-start = ((bf16[32,2,2560]{2,1,0:T(2,128)(2,1)}), bf16[32,2,2560]{2,1,0:T(2,128)(2,1)S(1)}, u32[]{:S(2)}, u32[]{:S(2)}) async-start(bf16[32,2,2560]{2,1,0:T(2,128)(2,1)} %reshape.387), calls=%async_computation | async-start | bytes 655360 | tf_op jit(solution)/shard_map/while/body/eval_jaxpr/all_to_all | solution.py:98
  747.6 13.4 %all-to-all-start.1 = ((bf16[32,2,2560]{2,1,0:T(2,128)(2,1)}), bf16[32,2,2560]{2,1,0:T(2,128)(2,1)S(1)}, u32[]{:S(2)}, u32[]{:S(2)}) async-start(bf16[32,2,2560]{2,1,0:T(2,128)(2,1)} %reshape.390), calls=%async_computation.1 | async-start | bytes 655360 | tf_op jit(solution)/shard_map/while/body/eval_jaxpr/all_to_all | solution.py:101
  766.7 4.5 copy-start.2
  771.4 10.2 %copy-start.10 = (s32[2,40]{1,0:T(2,128)S(1)}, s32[2,40]{1,0:T(2,128)}, u32[]{:S(2)}) copy-start(s32[2,40]{1,0:T(2,128)} %param.34) | copy-start | bytes 964
  772.2 12.2 %collective-permute-start = (bf16[12,1,8,256]{3,2,0,1:T(8,128)(2,1)S(1)}, bf16[12,1,8,256]{3,2,0,1:T(8,128)(2,1)S(1)}, u32[]{:S(2)}, u32[]{:S(2)}) collective-permute-start(bf16[12,1,8,256]{3,2,0,1:T(8,128)(2,1)S(1)} %get-tuple-element.343), channel_id=1, source_target_pairs={{0,4},{4,8},{8,12},{12,16},{16,20},{20,24},{24,28},{28,32},{32,36}... | collective-permute-start | bytes 147464 | tf_op jit(solution)/shard_map/ppermute | solution.py:22
  775.4 9.0 collective-permute-start.1
  947.7 48.8 %copy-start.3 = (f32[1,32,1440]{2,1,0:T(8,128)}, f32[1,32,1440]{2,1,0:T(8,128)S(1)}, u32[]{:S(2)}) copy-start(f32[1,32,1440]{2,1,0:T(8,128)S(1)} %get-tuple-element.267) | copy-start | bytes 552964
  947.7 40.6 %copy-start.16 = (f32[40]{0:T(128)S(1)}, f32[40]{0:T(128)}, u32[]{:S(2)}) copy-start(f32[40]{0:T(128)} %param.35) | copy-start | bytes 484
  948.2 40.7 %collective-permute-start.2 = (bf16[12,1,32,256]{3,2,0,1:T(8,128)(2,1)S(1)}, bf16[12,1,32,256]{3,2,0,1:T(8,128)(2,1)S(1)}, u32[]{:S(2)}, u32[]{:S(2)}) collective-permute-start(bf16[12,1,32,256]{3,2,0,1:T(8,128)(2,1)S(1)} %fusion.46), channel_id=1, source_target_pairs={{0,4},{4,8},{8,12},{12,16},{16,20},{20,24},{24,28},{28,32},{32,36}... | collective-permute-start | bytes 589832 | tf_op jit(solution)/shard_map/ppermute | solution.py:22
  986.3 9.1 collective-permute-start.3
  (19 other events, 21.0 us)
